TPU v7x, 32 devices: a whole 2x2x4 slice. The times are simulated.
32 devices in a mesh: row: 4 (over y, core), col: 8 (over z, x).
Axes of the slice: x: 2, y: 2, z: 4, core: 2. Of those that a mesh axis runs over, the one named last changes fastest.
Arguments:
- points: bfloat16 [65536, 512], P(('row', 'col')), may hold values from -6 to 6
- factor: bfloat16 [65536, 2048], P(('row', 'col')), may hold values from -0.078125 to 0.078125
- targets: bfloat16 [65536, 256], P(('row', 'col')), may hold values from -6 to 6
- pivot_slots: int32 [32, 32], P(('row', 'col')), may hold values from 0 to 2047, as said below
- pivot_counts: int32 [32], replicated, may hold values from 1 to 32, 512 in all
Outputs:
- new_columns: bfloat16 [512, 65536], P(None, ('row', 'col'))
- residual_next: float32 [65536, 256], P(('row', 'col'))
Inputs may be any that keep to these rules, and one draw needn't show every extreme that they name: `pivot_slots`: each row holds 32 different local row numbers; row d's first pivot_counts[d] entries are device d's pivots, the rest are unused. `pivot_counts`: the counts sum to 512; one of them is 32.
All inputs are finite; a program needn't handle non-finite values.
Results may differ from a plain program's by a relative error of at most 0.0029.
Values may be sent and summed in bfloat16 or wider, within the bound.
No kernel may reach another device: no remote copies, remote signals or barrier semaphores. Data moves between devices by JAX's collectives and lax.ppermute only.
A program may use at most 128 MiB of HBM per device.

v0:
```python
import jax
import jax.numpy as jnp
from jax import lax
from jax.sharding import PartitionSpec as P

BLOCK = 512
sharpness = 1.0
ridge_shift = 0.01
damping = 1.0
epsilon = 1e-06


def normalize(points):
    values = points.astype(jnp.float32)
    factor_scale = lax.rsqrt(jnp.mean(values * values, axis=1, keepdims=True) + epsilon)
    return (values * factor_scale).astype(jnp.bfloat16)


def kernel(left_rows, right_rows, feature_width):
    cosine = (
        lax.dot_general(
            left_rows, right_rows, (((1,), (1,)), ((), ())), preferred_element_type=jnp.float32
        )
        / feature_width
    )
    return jnp.exp(sharpness * (cosine - 1.0))


def compact_index(pivot_counts, block_size):
    owners_count = pivot_counts.shape[0]
    run_ends = jnp.cumsum(pivot_counts)
    run_starts = run_ends - pivot_counts
    position = jnp.arange(block_size, dtype=jnp.int32)
    owners = jnp.sum((position[:, None] >= run_ends[None, :]).astype(jnp.int32), axis=1)
    onehot = (owners[:, None] == jnp.arange(owners_count, dtype=jnp.int32)[None, :]).astype(
        jnp.int32
    )
    first_row = jnp.sum(onehot * run_starts[None, :], axis=1)
    return (owners, position - first_row)


def block_factor(pivot_scaled, pivot_factor):
    intersection = lax.dot_general(
        pivot_factor, pivot_factor, (((1,), (1,)), ((), ())), preferred_element_type=jnp.float32
    )
    diag_shift = ridge_shift + jnp.max(jnp.sum(jnp.abs(intersection), axis=1))
    ridged = (
        kernel(pivot_scaled, pivot_scaled, pivot_scaled.shape[1])
        - intersection
        + diag_shift * jnp.eye(intersection.shape[0], dtype=jnp.float32)
    )
    return jnp.linalg.cholesky(ridged)


def on_device(points, factor, targets, pivot_slots, pivot_counts):
    scaled = normalize(points)
    local_slots = pivot_slots[0]
    slot_cap = pivot_slots.shape[1]
    own_scaled = jnp.take(scaled, local_slots, axis=0)
    own_factor = jnp.take(factor, local_slots, axis=0)
    inner_scaled, inner_factor = (
        lax.all_gather(own_scaled, "col", axis=0, tiled=True),
        lax.all_gather(own_factor, "col", axis=0, tiled=True),
    )
    padded_scaled, padded_factor = (
        lax.all_gather(inner_scaled, "row", axis=0, tiled=True),
        lax.all_gather(inner_factor, "row", axis=0, tiled=True),
    )
    owners, slot_index = compact_index(pivot_counts, BLOCK)
    row_index = owners * slot_cap + slot_index
    pivot_scaled = jnp.take(padded_scaled, row_index, axis=0)
    pivot_factor = jnp.take(padded_factor, row_index, axis=0)
    lower_factor = block_factor(pivot_scaled, pivot_factor)
    downdated = kernel(pivot_scaled, scaled, scaled.shape[1]) - lax.dot_general(
        pivot_factor, factor, (((1,), (1,)), ((), ())), preferred_element_type=jnp.float32
    )
    new_columns = lax.linalg.triangular_solve(
        lower_factor, downdated, left_side=True, lower=True
    ).astype(jnp.bfloat16)
    cross_terms = jnp.concatenate(
        [
            lax.dot_general(
                factor, targets, (((0,), (0,)), ((), ())), preferred_element_type=jnp.float32
            ),
            lax.dot_general(
                new_columns, targets, (((1,), (0,)), ((), ())), preferred_element_type=jnp.float32
            ),
        ],
        axis=0,
    )
    col_norms = jnp.concatenate(
        [
            jnp.sum(jnp.square(factor.astype(jnp.float32)), axis=0),
            jnp.sum(jnp.square(new_columns.astype(jnp.float32)), axis=1),
        ],
        axis=0,
    )
    cross_whole, norm_whole = lax.psum((cross_terms, col_norms), ("row", "col"))
    coefficients = (cross_whole / (norm_whole + damping)[:, None]).astype(jnp.bfloat16)
    held_count = factor.shape[1]
    fitted = jnp.dot(factor, coefficients[:held_count], preferred_element_type=jnp.float32)
    fitted = fitted + lax.dot_general(
        new_columns,
        coefficients[held_count:],
        (((0,), (0,)), ((), ())),
        preferred_element_type=jnp.float32,
    )
    residual_next = targets.astype(jnp.float32) - fitted
    return (new_columns, residual_next)


def solution(mesh):
    return jax.shard_map(
        on_device,
        mesh=mesh,
        in_specs=(
            P(("row", "col"), None),
            P(("row", "col"), None),
            P(("row", "col"), None),
            P(("row", "col"), None),
            P(),
        ),
        out_specs=(P(None, ("row", "col")), P(("row", "col"), None)),
        check_vma=False,
    )
```

profile of v0, /device:TPU:0, one launch (start us, length us, event | category | flops | bytes accessed | tf_op | source)
XLA Modules:
  0.0 457.6 jit_solution(8331831617520132772)
XLA Ops:
  7.2 0.7 fusion.40
  7.9 0.7 compare_and_fusion
  8.5 5.2 %gather_fusion.2 = bf16[32,2048]{1,0:T(8,128)(2,1)S(1)} fusion(bf16[2048,2048]{1,0:T(8,128)(2,1)} %param.6, s32[1024]{0:T(1024)S(1)} %pad_clamp_fusion.1), kind=kCustom, calls=%fused_computation.2 | custom fusion | bytes 262272 | tf_op jit(solution)/shard_map/jit(_take)/gather | solution.py:60
  13.8 0.7 broadcast_select_fusion.6
  14.6 2.2 fusion
  17.3 0.6 gather_fusion
  18.0 35.1 %all_gather.12 = bf16[256,512]{1,0:T(8,128)(2,1)} all-gather(bf16[32,512]{1,0:T(8,128)(2,1)S(1)} %broadcast_select_fusion.7), channel_id=1, replica_groups=mesh['row'=4,'col'=8] {'col'}, dimensions={0}, use_global_device_ids=true | all-gather | bytes 294912 | tf_op jit(solution)/shard_map/all_gather | solution.py:62
  53.2 5.6 %all-gather.6.cloned.1.call-done = bf16[256,2048]{1,0:T(8,128)(2,1)} async-done(((bf16[32,2048]{1,0:T(8,128)(2,1)}), bf16[256,2048]{1,0:T(8,128)(2,1)}) %all-gather.6.cloned.1.call-update) | async-done | bytes 1048592 | tf_op jit(solution)/shard_map/all_gather | solution.py:63
  59.5 7.2 %fusion.51 = f32[2048,256]{1,0:T(8,128)} fusion(bf16[2048,2048]{1,0:T(8,128)(2,1)} %param.6, bf16[2048,256]{1,0:T(8,128)(2,1)S(1)} %copy-done.6), kind=kOutput, calls=%fused_computation.122 | convolution fusion | flops 2147483648 | bytes 11534336 | tf_op jit(solution)/shard_map/dot_general | solution.py:82
  66.7 9.0 %all-gather.4.cloned.1.call-done = bf16[1024,512]{1,0:T(8,128)(2,1)} async-done(((bf16[256,512]{1,0:T(8,128)(2,1)}), bf16[1024,512]{1,0:T(8,128)(2,1)}) %all-gather.4.cloned.1.call-update) | async-done | bytes 1048592 | tf_op jit(solution)/shard_map/all_gather | solution.py:66
  75.7 4.0 gather_fusion.1
  79.7 32.0 %all-gather.8.cloned.1.call-done = bf16[1024,2048]{1,0:T(8,128)(2,1)} async-done(((bf16[256,2048]{1,0:T(8,128)(2,1)}), bf16[1024,2048]{1,0:T(8,128)(2,1)}) %all-gather.8.cloned.1.call-update) | async-done | bytes 4194320 | tf_op jit(solution)/shard_map/all_gather | solution.py:67
  111.8 8.0 %gather_fusion.3 = bf16[512,2048]{1,0:T(8,128)(2,1)} fusion(bf16[1024,2048]{1,0:T(8,128)(2,1)} %all-gather.8.cloned.1.call-done, s32[1024]{0:T(1024)S(1)} %pad_clamp_fusion), kind=kCustom, calls=%fused_computation.3 | custom fusion | bytes 4196352 | tf_op jit(solution)/shard_map/jit(_take)/gather | solution.py:72
  119.7 3.7 abs_reduce_fusion
  123.5 9.9 %fusion.21 = f32[512,2048]{1,0:T(8,128)} fusion(bf16[2048,2048]{1,0:T(8,128)(2,1)} %param.6, bf16[512,2048]{1,0:T(8,128)(2,1)S(1)} %copy-done.4, pred[512]{0:T(512)(128)(4,1)S(1)} %compare_and_fusion.1), kind=kOutput, calls=%fused_computation.51 | convolution fusion | flops 4296015872 | bytes 14680576 | tf_op jit(solution)/shard_map/dot_general | solution.py:74
  133.3 1.3 copy.20
  134.6 2.1 fusion.17
  136.8 1.3 copy.21
  138.1 0.6 reduce_max.9
  139.3 1.4 add_multiply_fusion
  140.8 1.0 copy-done.3
  141.8 11.7 %cholesky.103 = f32[128,128]{1,0:T(8,128)S(1)} custom-call(f32[128,128]{1,0:T(8,128)S(1)} %cholesky.263), custom_call_target="Cholesky" | custom-call | tf_op jit(solution)/shard_map/jit(cholesky)/cholesky | solution.py:52
  153.7 9.8 %custom-call.30 = f32[1,128,128]{1,2,0:T(8,128)S(1)} custom-call(f32[1,128,128]{2,1,0:T(8,128)S(1)} %get-tuple-element.37), custom_call_target="InvertDiagBlocksLowerTriangular" | custom-call | tf_op jit(solution)/shard_map/jit(cholesky)/cholesky | solution.py:52
  163.5 1.2 constant_dynamic-update-slice_fusion.3
  164.7 1.3 convolution_subtract_fusion.2
  166.0 11.7 %cholesky.215 = f32[128,128]{1,0:T(8,128)S(1)} custom-call(f32[128,128]{1,0:T(8,128)S(1)} %cholesky.267), custom_call_target="Cholesky" | custom-call | tf_op jit(solution)/shard_map/jit(cholesky)/cholesky | solution.py:52
  177.8 10.2 %custom-call.31 = f32[1,128,128]{1,2,0:T(8,128)S(1)} custom-call(f32[1,128,128]{2,1,0:T(8,128)S(1)} %get-tuple-element.34), custom_call_target="InvertDiagBlocksLowerTriangular" | custom-call | tf_op jit(solution)/shard_map/jit(cholesky)/cholesky | solution.py:52
  188.3 1.3 convolution_subtract_fusion.3
  189.6 11.7 %cholesky.236 = f32[128,128]{1,0:T(8,128)S(1)} custom-call(f32[128,128]{1,0:T(8,128)S(1)} %cholesky.272), custom_call_target="Cholesky" | custom-call | tf_op jit(solution)/shard_map/jit(cholesky)/cholesky | solution.py:52
  201.3 0.7 compare_reduce_fusion.1
  202.0 9.8 %custom-call.32 = f32[1,128,128]{1,2,0:T(8,128)S(1)} custom-call(f32[1,128,128]{2,1,0:T(8,128)S(1)} %get-tuple-element.31), custom_call_target="InvertDiagBlocksLowerTriangular" | custom-call | tf_op jit(solution)/shard_map/jit(cholesky)/cholesky | solution.py:52
  212.0 1.2 convolution_subtract_fusion.4
  213.2 11.8 %cholesky.253 = f32[128,128]{1,0:T(8,128)S(1)} custom-call(f32[128,128]{1,0:T(8,128)S(1)} %convolution_subtract_fusion.4), custom_call_target="Cholesky" | custom-call | tf_op jit(solution)/shard_map/jit(cholesky)/cholesky | solution.py:52
  225.1 0.6 compare_reduce_fusion
  225.7 0.6 compare_reduce_fusion.2
  228.8 1.1 select_select_fusion
  229.9 13.6 %while.1 = (s32[]{:T(128)}, f32[512,512]{1,0:T(8,128)}, s32[4,2]{0,1:T(2,128)S(1)}, f32[4,128,128]{2,1,0:T(8,128)}, s32[]{:T(128)}) while((s32[]{:T(128)}, f32[512,512]{1,0:T(8,128)}, s32[4,2]{0,1:T(2,128)S(1)}, f32[4,128,128]{2,1,0:T(8,128)}, s32[]{:T(128)}) %tuple.39), condition=%wide.while_cond, body=%wide.while_body.sunk | while | flops 2 | bytes 132705 | solution.py:77
  230.0 0.5 fusion.67
  230.6 2.8 bitcast_dynamic-update-slice_fusion.2
  233.5 0.5 fusion.67
  234.0 2.8 bitcast_dynamic-update-slice_fusion.2
  237.4 2.8 bitcast_dynamic-update-slice_fusion.2
  240.8 2.7 bitcast_dynamic-update-slice_fusion.2
  243.6 40.1 %custom-call.33 = f32[4,128,128]{1,2,0:T(8,128)S(1)} custom-call(f32[4,128,128]{2,1,0:T(8,128)} %get-tuple-element.9), custom_call_target="InvertDiagBlocksLowerTriangular" | custom-call | tf_op jit(solution)/shard_map/triangular_solve | solution.py:77
  283.7 3.7 exponential_subtract_fusion
  287.4 1.1 fusion.50
  288.5 1.9 convolution_subtract_fusion.1
  290.4 1.0 fusion.49
  291.4 2.2 convolution_subtract_fusion
  293.6 1.0 fusion.48
  294.7 3.0 fusion.9
  297.7 1.1 convolution_convert_fusion
  298.8 0.6 multiply_reduce_fusion.1
  299.4 1.3 copy-done
  300.7 0.7 fusion.52
  301.7 1.7 pad_maximum_fusion
  303.4 0.9 copy.22
  304.3 5.1 %multiply_reduce_fusion = f32[2048]{0:T(1024)S(1)} fusion(bf16[2048,2048]{1,0:T(8,128)(2,1)} %param.6), kind=kLoop, calls=%fused_computation.6 | loop fusion | flops 12580864 | bytes 8396800 | tf_op jit(solution)/shard_map/reduce_sum | solution.py:93
  309.4 39.6 %psum.15 = f32[2560]{0:T(1024)S(1)} all-reduce(f32[2560]{0:T(1024)S(1)} %pad_maximum_fusion.2), channel_id=1, replica_groups=mesh['row'=4,'col'=8] {'row','col'}, use_global_device_ids=true, to_apply=%region_17.18 | all-reduce | flops 2560 | bytes 20480 | tf_op jit(solution)/shard_map/psum | solution.py:98
  349.0 91.1 %all-reduce.3.cloned.1.call-done = f32[2560,256]{1,0:T(8,128)} async-done(((f32[2560,256]{1,0:T(8,128)}), f32[2560,256]{1,0:T(8,128)}) %all-reduce.3.cloned.1.call-update) | async-done | bytes 2621456 | tf_op jit(solution)/shard_map/psum | solution.py:98
  440.1 2.1 divide_convert_fusion
  442.3 5.9 %convolution_bitcast_fusion = f32[2048,256]{0,1:T(8,128)S(1)} fusion(bf16[2048,2048]{1,0:T(8,128)(2,1)} %param.6, bf16[2560,256]{1,0:T(8,128)(2,1)S(1)} %divide_convert_fusion), kind=kOutput, calls=%fused_computation.21 | convolution fusion | flops 2147483648 | bytes 11534336 | tf_op jit(solution)/shard_map/dot_general | solution.py:101
  448.2 0.8 fusion.8
  449.0 1.8 copy.24
  (59 shorter events, 3.9 us)
Async XLA Ops:
  7.2 51.6 %all-gather.6.cloned.1.call-start = ((), (), s32[]{:S(2)}) async-start(), calls=%async_computation.1 | async-start | bytes 1179648 | tf_op jit(solution)/shard_map/all_gather | solution.py:63
  14.5 61.2 %all-gather.4.cloned.1.call-start = ((), (), s32[]{:S(2)}) async-start(), calls=%async_computation | async-start | bytes 1310720 | tf_op jit(solution)/shard_map/all_gather | solution.py:66
  14.6 2.3 copy-start.2
  16.8 42.1 %copy-start.8 = (s32[32]{0:T(128)S(1)}, s32[32]{0:T(128)}, u32[]{:S(2)}) copy-start(s32[32]{0:T(128)} %param.9) | copy-start | bytes 388
  16.9 42.7 %copy-start.6 = (bf16[2048,256]{1,0:T(8,128)(2,1)S(1)}, bf16[2048,256]{1,0:T(8,128)(2,1)}, u32[]{:S(2)}) copy-start(bf16[2048,256]{1,0:T(8,128)(2,1)} %param.7) | copy-start | bytes 3145732
  53.1 58.6 %all-gather.8.cloned.1.call-start = ((), (), s32[]{:S(2)}) async-start(), calls=%async_computation.2 | async-start | bytes 5242880 | tf_op jit(solution)/shard_map/all_gather | solution.py:67
  58.8 381.4 %all-reduce.3.cloned.1.call-start = ((), (), s32[]{:S(2)}) async-start(), calls=%async_computation.3 | async-start | bytes 5242880 | tf_op jit(solution)/shard_map/psum | solution.py:98
  119.7 3.8 copy-start.4
  140.8 1.0 copy-start.3
  297.7 3.0 copy-start.7
  299.4 1.3 copy-start
  299.4 2.3 copy-start.5
  442.3 5.9 %copy-start.1 = (bf16[512,2048]{1,0:T(8,128)(2,1)S(1)}, bf16[512,2048]{1,0:T(8,128)(2,1)}, u32[]{:S(2)}) copy-start(bf16[512,2048]{1,0:T(8,128)(2,1)} %copy-done) | copy-start | bytes 6291460
Sparse Core Ops, SparseCore 0:
  14.7 44.0 all-gather.5
  60.3 15.3 all-gather.3
  77.3 34.4 all-gather.7
  303.6 136.5 all-reduce.2
where the time goes:
time: 461 us; the launch traced here: 458 us
  waiting for transfers between devices  138 us (30%)
  other arithmetic  137 us (30%)
  blocking collectives  74.7 us (16%)
  matrix products  50.8 us (11%)
  local copies, waits for them, and re-layouts  39.5 us (9%)
  between operations  17.5 us (4%)
    psum x1, waiting for transfers between devices, on_device(): cross_whole, norm_whole = lax.psum((cross_terms, col_norms), ('row', 'col'))  91.1 us
    another operation x14, other arithmetic, block_factor(): return jnp.linalg.cholesky(ridged)  78.9 us
    another operation x3, other arithmetic, on_device(): lax.linalg.triangular_solve(lower_factor, downdated, left_side=True, lowe...  41.2 us
    psum x1, blocking collectives, on_device(): cross_whole, norm_whole = lax.psum((cross_terms, col_norms), ('row', 'col'))  39.6 us
    all_gather x1, blocking collectives, on_device(): lax.all_gather(own_scaled, 'col', axis=0, tiled=True)  35.1 us
    all_gather x1, waiting for transfers between devices, on_device(): lax.all_gather(inner_factor, 'row', axis=0, tiled=True)  32 us
    another operation x13, local copies, waits for them, and re-layouts  13.7 us
    another operation x7, matrix products, on_device(): lax.linalg.triangular_solve(lower_factor, downdated, left_side=True, lowe...  11.3 us
  transfers between devices with their start and end apart: 4, of which 4 were waited for; matrix products, arithmetic and copies ran while one was open for 5% of the time, Pallas kernels for 0%

commit v1 on v0

--- a/solution.py
+++ b/solution.py
@@ -8,6 +8,12 @@
 ridge_shift = 0.01
 damping = 1.0
 epsilon = 1e-06
+
+
+def _solve_forms(x_part, comm_axis, axis_key):
+    tmp = lax.psum(x_part, axis_name=comm_axis)
+    a_next = lax.psum(tmp, axis_key)
+    return a_next
 
 
 def normalize(points):
@@ -95,7 +101,7 @@
         ],
         axis=0,
     )
-    cross_whole, norm_whole = lax.psum((cross_terms, col_norms), ("row", "col"))
+    cross_whole, norm_whole = _solve_forms((cross_terms, col_norms), "col", "row")
     coefficients = (cross_whole / (norm_whole + damping)[:, None]).astype(jnp.bfloat16)
     held_count = factor.shape[1]
     fitted = jnp.dot(factor, coefficients[:held_count], preferred_element_type=jnp.float32)

time: 461 us -> 502 us (1.089)
  waiting for transfers between devices: 138 us -> 172 us
  blocking collectives: 74.7 us -> 81.7 us
    psum x1 -> x2, waiting for transfers between devices: 91.1 us -> 125 us  [the longest x1 116 us: _solve_forms(): tmp = lax.psum(x_part, axis_name=comm_axis)]
    psum x1 -> x2, blocking collectives: 39.6 us -> 46.7 us  [the longest x1 34.9 us: _solve_forms(): tmp = lax.psum(x_part, axis_name=comm_axis)]
  transfers between devices with their start and end apart: 4 -> 5, of which waited for: 4 -> 5; matrix products, arithmetic and copies ran while one was open for 5% -> 4% of each run, Pallas kernels for 0% -> 0%
where the time goes in v1:
time: 502 us; the launch traced here: 499 us
  waiting for transfers between devices  172 us (34%)
  other arithmetic  137 us (27%)
  blocking collectives  81.7 us (16%)
  matrix products  50.8 us (10%)
  local copies, waits for them, and re-layouts  39.5 us (8%)
  between operations  17.5 us (3%)
    psum x1, waiting for transfers between devices, _solve_forms(): tmp = lax.psum(x_part, axis_name=comm_axis)  116 us
    another operation x14, other arithmetic, block_factor(): return jnp.linalg.cholesky(ridged)  78.9 us
    another operation x3, other arithmetic, on_device(): lax.linalg.triangular_solve(lower_factor, downdated, left_side=True, lowe...  41.2 us
    all_gather x1, blocking collectives, on_device(): lax.all_gather(own_scaled, 'col', axis=0, tiled=True)  35.1 us
    psum x1, blocking collectives, _solve_forms(): tmp = lax.psum(x_part, axis_name=comm_axis)  34.9 us
    all_gather x1, waiting for transfers between devices, on_device(): lax.all_gather(inner_factor, 'row', axis=0, tiled=True)  32 us
    another operation x13, local copies, waits for them, and re-layouts  13.7 us
    psum x1, blocking collectives, _solve_forms(): a_next = lax.psum(tmp, axis_key)  11.8 us
  transfers between devices with their start and end apart: 5, of which 5 were waited for; matrix products, arithmetic and copies ran while one was open for 4% of the time, Pallas kernels for 0%

profile of v1, /device:TPU:0, one launch (start us, length us, event | category | flops | bytes accessed | tf_op | source)
XLA Modules:
  0.0 498.5 jit_solution(2001025210053254846)
XLA Ops:
  7.2 0.7 fusion.40
  7.9 0.7 compare_and_fusion
  8.5 5.2 %gather_fusion.2 = bf16[32,2048]{1,0:T(8,128)(2,1)S(1)} fusion(bf16[2048,2048]{1,0:T(8,128)(2,1)} %param.6, s32[1024]{0:T(1024)S(1)} %pad_clamp_fusion.1), kind=kCustom, calls=%fused_computation.2 | custom fusion | bytes 262272 | tf_op jit(solution)/shard_map/jit(_take)/gather | solution.py:66
  13.8 0.7 broadcast_select_fusion.6
  14.6 2.2 fusion
  17.3 0.6 gather_fusion
  18.0 35.1 %all_gather.12 = bf16[256,512]{1,0:T(8,128)(2,1)} all-gather(bf16[32,512]{1,0:T(8,128)(2,1)S(1)} %broadcast_select_fusion.7), channel_id=1, replica_groups=mesh['row'=4,'col'=8] {'col'}, dimensions={0}, use_global_device_ids=true | all-gather | bytes 294912 | tf_op jit(solution)/shard_map/all_gather | solution.py:68
  53.2 5.6 %all-gather.6.cloned.1.call-done = bf16[256,2048]{1,0:T(8,128)(2,1)} async-done(((bf16[32,2048]{1,0:T(8,128)(2,1)}), bf16[256,2048]{1,0:T(8,128)(2,1)}) %all-gather.6.cloned.1.call-update) | async-done | bytes 1048592 | tf_op jit(solution)/shard_map/all_gather | solution.py:69
  59.5 7.2 %fusion.51 = f32[2048,256]{1,0:T(8,128)} fusion(bf16[2048,2048]{1,0:T(8,128)(2,1)} %param.6, bf16[2048,256]{1,0:T(8,128)(2,1)S(1)} %copy-done.6), kind=kOutput, calls=%fused_computation.122 | convolution fusion | flops 2147483648 | bytes 11534336 | tf_op jit(solution)/shard_map/dot_general | solution.py:88
  66.7 9.0 %all-gather.4.cloned.1.call-done = bf16[1024,512]{1,0:T(8,128)(2,1)} async-done(((bf16[256,512]{1,0:T(8,128)(2,1)}), bf16[1024,512]{1,0:T(8,128)(2,1)}) %all-gather.4.cloned.1.call-update) | async-done | bytes 1048592 | tf_op jit(solution)/shard_map/all_gather | solution.py:72
  75.7 4.0 gather_fusion.1
  79.7 32.0 %all-gather.8.cloned.1.call-done = bf16[1024,2048]{1,0:T(8,128)(2,1)} async-done(((bf16[256,2048]{1,0:T(8,128)(2,1)}), bf16[1024,2048]{1,0:T(8,128)(2,1)}) %all-gather.8.cloned.1.call-update) | async-done | bytes 4194320 | tf_op jit(solution)/shard_map/all_gather | solution.py:73
  111.8 8.0 %gather_fusion.3 = bf16[512,2048]{1,0:T(8,128)(2,1)} fusion(bf16[1024,2048]{1,0:T(8,128)(2,1)} %all-gather.8.cloned.1.call-done, s32[1024]{0:T(1024)S(1)} %pad_clamp_fusion), kind=kCustom, calls=%fused_computation.3 | custom fusion | bytes 4196352 | tf_op jit(solution)/shard_map/jit(_take)/gather | solution.py:78
  119.7 3.7 abs_reduce_fusion
  123.5 9.9 %fusion.21 = f32[512,2048]{1,0:T(8,128)} fusion(bf16[2048,2048]{1,0:T(8,128)(2,1)} %param.6, bf16[512,2048]{1,0:T(8,128)(2,1)S(1)} %copy-done.4, pred[512]{0:T(512)(128)(4,1)S(1)} %compare_and_fusion.1), kind=kOutput, calls=%fused_computation.51 | convolution fusion | flops 4296015872 | bytes 14680576 | tf_op jit(solution)/shard_map/dot_general | solution.py:80
  133.3 1.3 copy.20
  134.6 2.1 fusion.17
  136.8 1.3 copy.21
  138.1 0.6 reduce_max.9
  139.3 1.4 add_multiply_fusion
  140.8 1.0 copy-done.3
  141.8 11.7 %cholesky.103 = f32[128,128]{1,0:T(8,128)S(1)} custom-call(f32[128,128]{1,0:T(8,128)S(1)} %cholesky.263), custom_call_target="Cholesky" | custom-call | tf_op jit(solution)/shard_map/jit(cholesky)/cholesky | solution.py:58
  153.7 9.8 %custom-call.30 = f32[1,128,128]{1,2,0:T(8,128)S(1)} custom-call(f32[1,128,128]{2,1,0:T(8,128)S(1)} %get-tuple-element.37), custom_call_target="InvertDiagBlocksLowerTriangular" | custom-call | tf_op jit(solution)/shard_map/jit(cholesky)/cholesky | solution.py:58
  163.5 1.2 constant_dynamic-update-slice_fusion.3
  164.7 1.3 convolution_subtract_fusion.2
  166.0 11.7 %cholesky.215 = f32[128,128]{1,0:T(8,128)S(1)} custom-call(f32[128,128]{1,0:T(8,128)S(1)} %cholesky.267), custom_call_target="Cholesky" | custom-call | tf_op jit(solution)/shard_map/jit(cholesky)/cholesky | solution.py:58
  177.8 10.2 %custom-call.31 = f32[1,128,128]{1,2,0:T(8,128)S(1)} custom-call(f32[1,128,128]{2,1,0:T(8,128)S(1)} %get-tuple-element.34), custom_call_target="InvertDiagBlocksLowerTriangular" | custom-call | tf_op jit(solution)/shard_map/jit(cholesky)/cholesky | solution.py:58
  188.3 1.3 convolution_subtract_fusion.3
  189.6 11.7 %cholesky.236 = f32[128,128]{1,0:T(8,128)S(1)} custom-call(f32[128,128]{1,0:T(8,128)S(1)} %cholesky.272), custom_call_target="Cholesky" | custom-call | tf_op jit(solution)/shard_map/jit(cholesky)/cholesky | solution.py:58
  201.3 0.7 compare_reduce_fusion.1
  202.0 9.8 %custom-call.32 = f32[1,128,128]{1,2,0:T(8,128)S(1)} custom-call(f32[1,128,128]{2,1,0:T(8,128)S(1)} %get-tuple-element.31), custom_call_target="InvertDiagBlocksLowerTriangular" | custom-call | tf_op jit(solution)/shard_map/jit(cholesky)/cholesky | solution.py:58
  212.0 1.2 convolution_subtract_fusion.4
  213.2 11.8 %cholesky.253 = f32[128,128]{1,0:T(8,128)S(1)} custom-call(f32[128,128]{1,0:T(8,128)S(1)} %convolution_subtract_fusion.4), custom_call_target="Cholesky" | custom-call | tf_op jit(solution)/shard_map/jit(cholesky)/cholesky | solution.py:58
  225.1 0.6 compare_reduce_fusion
  225.7 0.6 compare_reduce_fusion.2
  228.8 1.1 select_select_fusion
  229.9 13.6 %while.1 = (s32[]{:T(128)}, f32[512,512]{1,0:T(8,128)}, s32[4,2]{0,1:T(2,128)S(1)}, f32[4,128,128]{2,1,0:T(8,128)}, s32[]{:T(128)}) while((s32[]{:T(128)}, f32[512,512]{1,0:T(8,128)}, s32[4,2]{0,1:T(2,128)S(1)}, f32[4,128,128]{2,1,0:T(8,128)}, s32[]{:T(128)}) %tuple.39), condition=%wide.while_cond, body=%wide.while_body.sunk | while | flops 2 | bytes 132705 | solution.py:83
  230.6 2.8 bitcast_dynamic-update-slice_fusion.2
  234.0 2.8 bitcast_dynamic-update-slice_fusion.2
  237.4 2.8 bitcast_dynamic-update-slice_fusion.2
  240.8 2.7 bitcast_dynamic-update-slice_fusion.2
  243.6 40.1 %custom-call.33 = f32[4,128,128]{1,2,0:T(8,128)S(1)} custom-call(f32[4,128,128]{2,1,0:T(8,128)} %get-tuple-element.9), custom_call_target="InvertDiagBlocksLowerTriangular" | custom-call | tf_op jit(solution)/shard_map/triangular_solve | solution.py:83
  283.7 3.7 exponential_subtract_fusion
  287.4 1.1 fusion.50
  288.5 1.9 convolution_subtract_fusion.1
  290.4 1.0 fusion.49
  291.4 2.2 convolution_subtract_fusion
  293.6 1.0 fusion.48
  294.7 3.0 fusion.9
  297.7 1.1 convolution_convert_fusion
  298.8 0.6 multiply_reduce_fusion.1
  299.4 1.3 copy-done
  300.7 0.7 fusion.52
  301.7 1.7 pad_maximum_fusion
  303.5 116.1 %all-reduce.4.cloned.1.call-done = f32[2560,256]{1,0:T(8,128)} async-done(((f32[2560,256]{1,0:T(8,128)}), f32[2560,256]{1,0:T(8,128)}) %all-reduce.4.cloned.1.call-update) | async-done | bytes 2621456 | tf_op jit(solution)/shard_map/psum | solution.py:14
  419.7 0.9 copy.22
  420.5 5.1 %multiply_reduce_fusion = f32[2048]{0:T(1024)S(1)} fusion(bf16[2048,2048]{1,0:T(8,128)(2,1)} %param.6), kind=kLoop, calls=%fused_computation.6 | loop fusion | flops 12580864 | bytes 8396800 | tf_op jit(solution)/shard_map/reduce_sum | solution.py:99
  425.6 34.9 %psum.30 = f32[2560]{0:T(1024)S(1)} all-reduce(f32[2560]{0:T(1024)S(1)} %pad_maximum_fusion.2), channel_id=1, replica_groups=mesh['row'=4,'col'=8] {'col'}, use_global_device_ids=true, to_apply=%region_18.19 | all-reduce | flops 2560 | bytes 20480 | tf_op jit(solution)/shard_map/psum | solution.py:14
  460.6 11.8 %psum.31 = f32[2560]{0:T(1024)S(1)} all-reduce(f32[2560]{0:T(1024)S(1)} %psum.30), channel_id=1, replica_groups=mesh['row'=4,'col'=8] {'row'}, use_global_device_ids=true, to_apply=%region_19.20 | all-reduce | flops 2560 | bytes 20480 | tf_op jit(solution)/shard_map/psum | solution.py:15
  472.3 8.8 %all-reduce.6.cloned.1.call-done = f32[2560,256]{1,0:T(8,128)} async-done(((f32[2560,256]{1,0:T(8,128)}), f32[2560,256]{1,0:T(8,128)}) %all-reduce.6.cloned.1.call-update) | async-done | bytes 2621456 | tf_op jit(solution)/shard_map/psum | solution.py:15
  481.1 2.1 divide_convert_fusion
  483.3 5.9 %convolution_bitcast_fusion = f32[2048,256]{0,1:T(8,128)S(1)} fusion(bf16[2048,2048]{1,0:T(8,128)(2,1)} %param.6, bf16[2560,256]{1,0:T(8,128)(2,1)S(1)} %divide_convert_fusion), kind=kOutput, calls=%fused_computation.21 | convolution fusion | flops 2147483648 | bytes 11534336 | tf_op jit(solution)/shard_map/dot_general | solution.py:107
  489.2 0.8 fusion.8
  490.0 1.8 copy.24
  (63 shorter events, 5.0 us)
Async XLA Ops:
  7.2 51.6 %all-gather.6.cloned.1.call-start = ((), (), s32[]{:S(2)}) async-start(), calls=%async_computation.1 | async-start | bytes 1179648 | tf_op jit(solution)/shard_map/all_gather | solution.py:69
  14.5 61.2 %all-gather.4.cloned.1.call-start = ((), (), s32[]{:S(2)}) async-start(), calls=%async_computation | async-start | bytes 1310720 | tf_op jit(solution)/shard_map/all_gather | solution.py:72
  14.6 2.3 copy-start.2
  16.8 42.1 %copy-start.8 = (s32[32]{0:T(128)S(1)}, s32[32]{0:T(128)}, u32[]{:S(2)}) copy-start(s32[32]{0:T(128)} %param.9) | copy-start | bytes 388
  16.9 42.7 %copy-start.6 = (bf16[2048,256]{1,0:T(8,128)(2,1)S(1)}, bf16[2048,256]{1,0:T(8,128)(2,1)}, u32[]{:S(2)}) copy-start(bf16[2048,256]{1,0:T(8,128)(2,1)} %param.7) | copy-start | bytes 3145732
  53.1 58.6 %all-gather.8.cloned.1.call-start = ((), (), s32[]{:S(2)}) async-start(), calls=%async_computation.2 | async-start | bytes 5242880 | tf_op jit(solution)/shard_map/all_gather | solution.py:73
  58.8 360.9 %all-reduce.4.cloned.1.call-start = ((), (), s32[]{:S(2)}) async-start(), calls=%async_computation.3 | async-start | bytes 5242880 | tf_op jit(solution)/shard_map/psum | solution.py:14
  119.7 3.8 copy-start.4
  140.8 1.0 copy-start.3
  297.7 3.0 copy-start.7
  299.4 1.3 copy-start
  299.4 2.3 copy-start.5
  303.4 177.6 %all-reduce.6.cloned.1.call-start = ((), (), s32[]{:S(2)}) async-start(), calls=%async_computation.4 | async-start | bytes 5242880 | tf_op jit(solution)/shard_map/psum | solution.py:15
  483.2 5.9 %copy-start.1 = (bf16[512,2048]{1,0:T(8,128)(2,1)S(1)}, bf16[512,2048]{1,0:T(8,128)(2,1)}, u32[]{:S(2)}) copy-start(bf16[512,2048]{1,0:T(8,128)(2,1)} %copy-done) | copy-start | bytes 6291460
Sparse Core Ops, SparseCore 0:
  14.7 44.0 all-gather.5
  60.3 15.3 all-gather.3
  77.3 34.4 all-gather.7
  303.6 116.0 all-reduce.3
  421.8 59.1 all-reduce.5
